TPU v7x, 256 devices: a whole 4x4x8 slice. The times are simulated.
256 devices in a mesh: strata: 16 (over z_lo, x), users: 16 (over y, z_hi, core).
Axes of the slice: x: 4, y: 4, z: 8 (z_hi: 2, z_lo: 4; z = z_hi * 4 + z_lo), core: 2. Of those that a mesh axis runs over, the one named last changes fastest.
Arguments:
- user_factors: float32 [524288, 256], P(('strata', 'users')), may hold values from -1.5 to 1.5
- item_factors: float32 [16384, 256], P(('strata', 'users')), may hold values from -1.5 to 1.5
- tile_rows: int32 [16, 16, 2, 64], P('strata', 'users'), may hold values from 0 to 15, as said below
- tile_columns: int32 [16, 16, 2, 64], P('strata', 'users'), may hold values from 0 to 7, as said below
- tile_counts: int32 [16, 16, 2], P('strata', 'users'), may hold values from 8 to 64, as said below
- ratings: int32 [16, 16, 2, 64, 128, 128], P('strata', 'users'), may hold values from 0 to 5
Outputs:
- updated_users: float32 [524288, 256], P(('strata', 'users'))
- updated_items: float32 [16384, 256], P(('strata', 'users'))
Inputs may be any that keep to these rules, and one draw needn't show every extreme that they name: `tile_rows`: row tile of each slot within the device's users. `tile_columns`: item tile of each slot within the step's item block; a device's slots of one step name distinct pairs of user tile and item tile, padding slots included. `tile_counts`: in every step some device uses all 64 slots.
All inputs are finite; a program needn't handle non-finite values.
Results may differ from a plain program's by a relative error of at most 0.0004.
Values may be sent and summed in bfloat16 or wider, within the bound.
A program may use at most 128 MiB of HBM per device.

v0:
```python
import jax
import jax.numpy as jnp
from jax import lax
from jax.sharding import PartitionSpec as P


def from_behind(block, axis, distance):
    devices = range(lax.axis_size(axis))
    route = [((i - distance) % len(devices), i) for i in devices]
    return lax.ppermute(block, axis, route)


def gradients(user_low, block_low, row_blocks, column_blocks, count, rating_tiles):
    tile_size = rating_tiles.shape[-1]
    factor_width = user_low.shape[1]
    row_tiles = user_low.shape[0] // tile_size
    item_tiles = block_low.shape[0] // tile_size
    slot_count = row_blocks.shape[0]
    user_tiles = user_low.reshape(row_tiles, tile_size, factor_width)[row_blocks]
    item_tiles_now = block_low.reshape(item_tiles, tile_size, factor_width)[column_blocks]
    predicted = jnp.einsum(
        "mik,mjk->mij", user_tiles, item_tiles_now, preferred_element_type=jnp.float32
    )
    in_list = jnp.arange(slot_count) < count
    observed = (rating_tiles > 0) & in_list[:, None, None]
    residual = jnp.where(observed, rating_tiles.astype(jnp.float32) - predicted, 0.0).astype(
        jnp.bfloat16
    )
    user_terms = jnp.einsum(
        "mij,mjk->mik", residual, item_tiles_now, preferred_element_type=jnp.float32
    )
    item_terms = jnp.einsum(
        "mij,mik->mjk", residual, user_tiles, preferred_element_type=jnp.float32
    )
    row_select = (row_blocks[:, None] == jnp.arange(row_tiles)[None, :]).astype(jnp.float32)
    column_select = (column_blocks[:, None] == jnp.arange(item_tiles)[None, :]).astype(jnp.float32)
    user_grad = jnp.einsum("mr,mik->rik", row_select, user_terms, precision=lax.Precision.HIGHEST)
    item_grad = jnp.einsum(
        "mr,mik->rik", column_select, item_terms, precision=lax.Precision.HIGHEST
    )
    return (user_grad.reshape(-1, factor_width), item_grad.reshape(-1, factor_width))


def shards(user_factors, item_factors, tile_rows, tile_columns, tile_counts, ratings):
    row_lists = tile_rows[0, 0]
    column_lists = tile_columns[0, 0]
    count_lists = tile_counts[0, 0]
    rating_lists = ratings[0, 0]
    step_total = rating_lists.shape[0]
    users_now = user_factors
    held_items = lax.all_gather(item_factors, "users", axis=0, tiled=True)
    for step_index in range(step_total):
        user_grad, item_grad = gradients(
            users_now.astype(jnp.bfloat16),
            held_items.astype(jnp.bfloat16),
            row_lists[step_index],
            column_lists[step_index],
            count_lists[step_index],
            rating_lists[step_index],
        )
        summed_grads = lax.psum(item_grad, "users")
        users_now = users_now + 0.01 * (user_grad - 0.05 * users_now)
        held_items = held_items + 0.003 * (summed_grads - 0.05 * held_items)
        if step_index < step_total - 1:
            held_items = from_behind(held_items, "strata", 1)
    own_rows = item_factors.shape[0]
    items_out = lax.dynamic_slice_in_dim(
        held_items, lax.axis_index("users") * own_rows, own_rows, 0
    )
    return (users_now, items_out)


def solution(mesh):
    placed = (
        P(("strata", "users"), None),
        P(("strata", "users"), None),
        P("strata", "users", None, None),
        P("strata", "users", None, None),
        P("strata", "users", None),
        P("strata", "users", None, None, None, None),
    )
    return jax.shard_map(
        shards,
        mesh=mesh,
        in_specs=placed,
        out_specs=(P(("strata", "users"), None), P(("strata", "users"), None)),
        check_vma=False,
    )
```

profile of v0, /device:TPU:1, one launch (start us, length us, event | category | flops | bytes accessed | tf_op | source)
XLA Modules:
  0.0 504.5 jit_solution(3911407407354205349)
XLA Ops:
  7.9 1.7 convert_element_type.36
  10.4 2.8 gather_fusion
  14.5 56.1 %all-gather.2.cloned.1.call-done = f32[1024,256]{1,0:T(8,128)} async-done(((f32[64,256]{1,0:T(8,128)}), f32[1024,256]{1,0:T(8,128)}) %all-gather.2.cloned.1.call-update) | async-done | bytes 1048592 | tf_op jit(solution)/shard_map/all_gather | solution.py:51
  70.6 1.3 convert_element_type.37
  71.9 2.8 gather_fusion.1
  74.7 6.1 %fusion.11 = bf16[64,128,128]{2,1,0:T(8,128)(2,1)S(1)} fusion(s32[1,1,2,64,128,128]{5,4,3,2,1,0:T(8,128)} %param.11, bf16[64,128,256]{2,1,0:T(8,128)(2,1)} %gather_fusion, bf16[64,128,256]{2,1,0:T(8,128)(2,1)} %gather_fusion.1, pred[64]{0:T(512)(128)(4,1)S(1)} %iota_compare_fusion.5), kind=kOutput, calls=%fused_computation.17 | convolution fusion | flops 543162368 | bytes 14680128 | tf_op jit(solution)/shard_map/mik,mjk->mij/dot_general | solution.py:21
  80.8 1.3 fusion.37
  82.1 7.5 %fusion.4 = f32[8,128,256]{2,0,1:T(8,128)S(1)} fusion(f32[64,128,256]{2,1,0:T(8,128)S(1)} %fusion.37, s32[64]{0:T(128)S(1)} %get-tuple-element.3), kind=kOutput, calls=%fused_computation.8 | convolution fusion | flops 201327104 | bytes 9437440 | tf_op jit(solution)/shard_map/mr,mik->rik/dot_general | solution.py:38
  89.6 1.3 copy.9
  90.9 12.9 %all-reduce.5.cloned.1.call-start = ((), (), s32[]{:S(2)}) async-start(), calls=%async_computation.2 | async-start | bytes 2097152 | tf_op jit(solution)/shard_map/psum | solution.py:61
  104.5 6.8 %fusion.36 = f32[64,128,256]{2,1,0:T(8,128)} fusion(bf16[64,128,128]{2,1,0:T(8,128)(2,1)S(1)} %fusion.11, bf16[64,128,256]{2,1,0:T(8,128)(2,1)} %gather_fusion.1), kind=kOutput, calls=%fused_computation.62 | convolution fusion | flops 536870912 | bytes 14680064 | tf_op jit(solution)/shard_map/mij,mjk->mik/dot_general | solution.py:29
  111.3 155.3 %all-reduce.3.cloned.1.call-done = f32[1024,256]{1,0:T(8,128)} async-done(((f32[1024,256]{1,0:T(8,128)}), f32[1024,256]{1,0:T(8,128)}) %all-reduce.3.cloned.1.call-update) | async-done | bytes 1048592 | tf_op jit(solution)/shard_map/psum | solution.py:61
  266.6 2.4 multiply_add_fusion
  269.0 1.4 collective-permute-start
  270.4 10.7 %fusion.6 = f32[16,128,256]{2,0,1:T(8,128)S(1)} fusion(f32[64,128,256]{2,1,0:T(8,128)} %fusion.36, s32[64]{0:T(128)S(1)} %get-tuple-element.5), kind=kOutput, calls=%fused_computation.10 | convolution fusion | flops 402654208 | bytes 10486016 | tf_op jit(solution)/shard_map/mr,mik->rik/dot_general | solution.py:37
  281.1 1.2 copy.8
  282.3 1.3 copy-done.4
  284.1 2.8 gather_fusion.2
  286.8 9.7 %collective-permute-done = f32[1024,256]{1,0:T(8,128)} collective-permute-done((f32[1024,256]{1,0:T(8,128)}, f32[1024,256]{1,0:T(8,128)}, u32[]{:S(2)}, u32[]{:S(2)}) %collective-permute-start) | collective-permute-done | bytes 1048608 | tf_op jit(solution)/shard_map/ppermute | solution.py:10
  296.5 1.3 convert_element_type.42
  297.8 2.8 gather_fusion.3
  300.6 6.1 %fusion.9 = bf16[64,128,128]{2,1,0:T(8,128)(2,1)S(1)} fusion(s32[1,1,2,64,128,128]{5,4,3,2,1,0:T(8,128)} %param.11, bf16[64,128,256]{2,1,0:T(8,128)(2,1)} %gather_fusion.2, bf16[64,128,256]{2,1,0:T(8,128)(2,1)} %gather_fusion.3, pred[64]{0:T(512)(128)(4,1)S(1)} %iota_compare_fusion.4), kind=kOutput, calls=%fused_computation.14 | convolution fusion | flops 543162368 | bytes 14680128 | tf_op jit(solution)/shard_map/mik,mjk->mij/dot_general | solution.py:21
  306.7 1.3 fusion.39
  308.0 0.9 copy-done.2
  308.9 4.5 fusion.38
  313.4 7.7 %fusion = f32[8,128,256]{2,0,1:T(8,128)S(1)} fusion(f32[64,128,256]{2,1,0:T(8,128)S(1)} %fusion.39, s32[64]{0:T(128)S(1)} %get-tuple-element.2), kind=kOutput, calls=%fused_computation.4 | convolution fusion | flops 201327104 | bytes 9437440 | tf_op jit(solution)/shard_map/mr,mik->rik/dot_general | solution.py:38
  321.0 1.3 copy.11
  322.4 10.7 %fusion.2 = f32[16,128,256]{2,0,1:T(8,128)S(1)} fusion(f32[64,128,256]{2,1,0:T(8,128)} %fusion.38, s32[64]{0:T(128)S(1)} %get-tuple-element.4), kind=kOutput, calls=%fused_computation.6 | convolution fusion | flops 402654208 | bytes 10486016 | tf_op jit(solution)/shard_map/mr,mik->rik/dot_general | solution.py:37
  333.1 1.2 copy.10
  334.7 1.9 fusion.13
  336.5 159.6 %all-reduce.5.cloned.1.call-done = f32[1024,256]{1,0:T(8,128)} async-done(((f32[1024,256]{1,0:T(8,128)}), f32[1024,256]{1,0:T(8,128)}) %all-reduce.5.cloned.1.call-update) | async-done | bytes 1048592 | tf_op jit(solution)/shard_map/psum | solution.py:61
  496.1 1.5 fusion.18
  (34 shorter events, 4.3 us)
Async XLA Ops:
  7.2 63.5 %all-gather.2.cloned.1.call-start = ((), (), s32[]{:S(2)}) async-start(), calls=%async_computation | async-start | bytes 1114112 | tf_op jit(solution)/shard_map/all_gather | solution.py:51
  7.9 258.7 %all-reduce.3.cloned.1.call-start = ((), (), s32[]{:S(2)}) async-start(), calls=%async_computation.1 | async-start | bytes 2097152 | tf_op jit(solution)/shard_map/psum | solution.py:61
  10.4 2.8 copy-start.9
  10.4 4.0 copy-start.7
  74.7 6.1 %copy-start = (bf16[64,128,256]{2,1,0:T(8,128)(2,1)S(1)}, bf16[64,128,256]{2,1,0:T(8,128)(2,1)}, u32[]{:S(2)}) copy-start(bf16[64,128,256]{2,1,0:T(8,128)(2,1)} %gather_fusion) | copy-start | bytes 12582916
  82.1 22.4 %copy-start.8 = (s32[1,1,2,64]{3,2,1,0:T(2,128)S(1)}, s32[1,1,2,64]{3,2,1,0:T(2,128)}, u32[]{:S(2)}) copy-start(s32[1,1,2,64]{3,2,1,0:T(2,128)} %param.8) | copy-start | bytes 1540
  90.9 405.2 %all-reduce.5.cloned.1.call-start = ((), (), s32[]{:S(2)}) async-start(), calls=%async_computation.2 | async-start | bytes 2097152 | tf_op jit(solution)/shard_map/psum | solution.py:61
  104.5 162.1 %copy-start.6 = (f32[1024,256]{1,0:T(8,128)S(1)}, f32[1024,256]{1,0:T(8,128)}, u32[]{:S(2)}) copy-start(f32[1024,256]{1,0:T(8,128)} %all-gather.2.cloned.1.call-done) | copy-start | bytes 3145732
  269.0 27.5 %collective-permute-start = (f32[1024,256]{1,0:T(8,128)}, f32[1024,256]{1,0:T(8,128)}, u32[]{:S(2)}, u32[]{:S(2)}) collective-permute-start(f32[1024,256]{1,0:T(8,128)} %multiply_add_fusion), channel_id=1, source_target_pairs={{240,0},{0,16},{16,32},{32,48},{48,64},{64,80},{80,96},{96,112},{1... | collective-permute-start | bytes 3145736 | tf_op jit(solution)/shard_map/ppermute | solution.py:10
  281.1 2.6 copy-start.3
  282.3 1.3 copy-start.4
  300.6 6.1 %copy-start.1 = (bf16[64,128,256]{2,1,0:T(8,128)(2,1)S(1)}, bf16[64,128,256]{2,1,0:T(8,128)(2,1)}, u32[]{:S(2)}) copy-start(bf16[64,128,256]{2,1,0:T(8,128)(2,1)} %gather_fusion.2) | copy-start | bytes 12582916
  306.7 2.2 copy-start.2
  333.1 1.6 copy-start.5
Sparse Core Ops, SparseCore 0:
  10.7 59.8 all-gather.1
  91.0 175.5 all-reduce.2
  322.5 173.5 all-reduce.4
where the time goes:
time: 513 us; the launch traced here: 505 us
  waiting for transfers between devices  381 us (74%)
  matrix products  62.6 us (12%)
  local copies, waits for them, and re-layouts  19.3 us (4%)
  between operations  14.4 us (3%)
  starting transfers between devices  14.3 us (3%)
  other arithmetic  12.5 us (2%)
    psum x2, waiting for transfers between devices, shards(): summed_grads = lax.psum(item_grad, 'users')  315 us
    all_gather x1, waiting for transfers between devices, shards(): held_items = lax.all_gather(item_factors, 'users', axis=0, tiled=True)  56.1 us
    dot_general x2, matrix products, gradients(): jnp.einsum('mr,mik->rik', row_select, user_terms, precision=lax.Precision...  21.4 us
    dot_general x2, matrix products, gradients(): jnp.einsum('mr,mik->rik', column_select, item_terms, precision=lax.Precis...  15.2 us
    psum x2, starting transfers between devices, shards(): summed_grads = lax.psum(item_grad, 'users')  12.9 us
    dot_general x2, matrix products, gradients(): jnp.einsum('mik,mjk->mij', user_tiles, item_tiles_now, preferred_element_...  12.2 us
    dot_general x2, matrix products, gradients(): jnp.einsum('mij,mjk->mik', residual, item_tiles_now, preferred_element_ty...  11.3 us
  transfers between devices with their start and end apart: 4, of which 4 were waited for; matrix products, arithmetic and copies ran while one was open for 8% of the time, Pallas kernels for 0%

commit v1 on v0

--- a/solution.py
+++ b/solution.py
@@ -1,7 +1,18 @@
+import functools
 import jax
 import jax.numpy as jnp
 from jax import lax
 from jax.sharding import PartitionSpec as P
+
+
+def cycles_open(buf, row_axis):
+    mid_arr = jnp.concatenate(
+        lax.all_to_all(jnp.stack(lax.axis_size(row_axis) * [buf]), row_axis, 0, 0), axis=0
+    )
+    return mid_arr
+
+
+make_ways = functools.partial(cycles_open, row_axis="users")
 
 
 def from_behind(block, axis, distance):
@@ -48,7 +59,7 @@
     rating_lists = ratings[0, 0]
     step_total = rating_lists.shape[0]
     users_now = user_factors
-    held_items = lax.all_gather(item_factors, "users", axis=0, tiled=True)
+    held_items = make_ways(item_factors)
     for step_index in range(step_total):
         user_grad, item_grad = gradients(
             users_now.astype(jnp.bfloat16),

time: 513 us -> 497 us (0.969)
  waiting for transfers between devices: 381 us -> 352 us
  starting transfers between devices: 14.3 us -> 26.9 us
    all_gather x1 -> x0, waiting for transfers between devices: 56.1 us -> none  [shards(): held_items = lax.all_gather(item_factors, 'users', axis=0, tiled=True)]
    all_to_all x0 -> x1, waiting for transfers between devices: none -> 17.8 us  [cycles_open(): lax.all_to_all(jnp.stack(lax.axis_size(row_axis) * [buf]), row_axis, 0, 0)]
    all_to_all x0 -> x1, starting transfers between devices: none -> 12.6 us  [cycles_open(): lax.all_to_all(jnp.stack(lax.axis_size(row_axis) * [buf]), row_axis, 0, 0)]
    psum x2, waiting for transfers between devices: 315 us -> 324 us  [shards(): summed_grads = lax.psum(item_grad, 'users')]
where the time goes in v1:
time: 497 us; the launch traced here: 488 us
  waiting for transfers between devices  352 us (71%)
  matrix products  62.4 us (13%)
  starting transfers between devices  26.9 us (5%)
  local copies, waits for them, and re-layouts  21.4 us (4%)
  between operations  14.7 us (3%)
  other arithmetic  10.5 us (2%)
    psum x2, waiting for transfers between devices, shards(): summed_grads = lax.psum(item_grad, 'users')  324 us
    dot_general x2, matrix products, gradients(): jnp.einsum('mr,mik->rik', row_select, user_terms, precision=lax.Precision...  21.4 us
    all_to_all x1, waiting for transfers between devices, cycles_open(): lax.all_to_all(jnp.stack(lax.axis_size(row_axis) * [buf]), row_axis, 0, 0)  17.8 us
    dot_general x2, matrix products, gradients(): jnp.einsum('mr,mik->rik', column_select, item_terms, precision=lax.Precis...  15.2 us
    psum x2, starting transfers between devices, shards(): summed_grads = lax.psum(item_grad, 'users')  12.9 us
    all_to_all x1, starting transfers between devices, cycles_open(): lax.all_to_all(jnp.stack(lax.axis_size(row_axis) * [buf]), row_axis, 0, 0)  12.6 us
    dot_general x2, matrix products, gradients(): jnp.einsum('mik,mjk->mij', user_tiles, item_tiles_now, preferred_element_...  12.2 us
    dot_general x2, matrix products, gradients(): jnp.einsum('mij,mjk->mik', residual, item_tiles_now, preferred_element_ty...  11.1 us
  transfers between devices with their start and end apart: 4, of which 4 were waited for; matrix products, arithmetic and copies ran while one was open for 8% of the time, Pallas kernels for 0%

profile of v1, /device:TPU:1, one launch (start us, length us, event | category | flops | bytes accessed | tf_op | source)
XLA Modules:
  0.0 487.6 jit_solution(10158579715231001767)
XLA Ops:
  7.2 2.1 stack.2
  9.3 12.6 %all-to-all-start = ((f32[16,64,256]{2,1,0:T(8,128)}), f32[16,64,256]{2,1,0:T(8,128)}, u32[]{:S(2)}, u32[]{:S(2)}) async-start(f32[16,64,256]{2,1,0:T(8,128)} %stack.2), calls=%async_computation | async-start | bytes 2097152 | tf_op jit(solution)/shard_map/all_to_all | solution.py:10
  22.1 2.8 gather_fusion
  26.1 17.8 %all-to-all-done = f32[16,64,256]{2,1,0:T(8,128)} async-done(((f32[16,64,256]{2,1,0:T(8,128)}), f32[16,64,256]{2,1,0:T(8,128)}, u32[]{:S(2)}, u32[]{:S(2)}) %all-to-all-start) | async-done | bytes 1048608 | tf_op jit(solution)/shard_map/all_to_all | solution.py:10
  43.9 1.3 convert_element_type.41
  45.2 2.8 gather_fusion.1
  48.0 6.1 %fusion.11 = bf16[64,128,128]{2,1,0:T(8,128)(2,1)S(1)} fusion(s32[1,1,2,64,128,128]{5,4,3,2,1,0:T(8,128)} %param.11, bf16[64,128,256]{2,1,0:T(8,128)(2,1)} %gather_fusion, bf16[64,128,256]{2,1,0:T(8,128)(2,1)} %gather_fusion.1, pred[64]{0:T(512)(128)(4,1)S(1)} %iota_compare_fusion.5), kind=kOutput, calls=%fused_computation.17 | convolution fusion | flops 543162368 | bytes 14680128 | tf_op jit(solution)/shard_map/mik,mjk->mij/dot_general | solution.py:32
  54.1 1.3 fusion.39
  55.4 7.5 %fusion.4 = f32[8,128,256]{2,0,1:T(8,128)S(1)} fusion(f32[64,128,256]{2,1,0:T(8,128)S(1)} %fusion.39, s32[64]{0:T(128)S(1)} %get-tuple-element.3), kind=kOutput, calls=%fused_computation.8 | convolution fusion | flops 201327104 | bytes 9437440 | tf_op jit(solution)/shard_map/mr,mik->rik/dot_general | solution.py:49
  62.9 1.3 copy.9
  64.2 12.9 %all-reduce.5.cloned.1.call-start = ((), (), s32[]{:S(2)}) async-start(), calls=%async_computation.2 | async-start | bytes 2097152 | tf_op jit(solution)/shard_map/psum | solution.py:72
  77.8 6.7 %fusion.38 = f32[64,128,256]{2,1,0:T(8,128)} fusion(bf16[64,128,128]{2,1,0:T(8,128)(2,1)S(1)} %fusion.11, bf16[64,128,256]{2,1,0:T(8,128)(2,1)} %gather_fusion.1), kind=kOutput, calls=%fused_computation.65 | convolution fusion | flops 536870912 | bytes 14680064 | tf_op jit(solution)/shard_map/mij,mjk->mik/dot_general | solution.py:40
  84.5 164.3 %all-reduce.3.cloned.1.call-done = f32[1024,256]{1,0:T(8,128)} async-done(((f32[1024,256]{1,0:T(8,128)}), f32[1024,256]{1,0:T(8,128)}) %all-reduce.3.cloned.1.call-update) | async-done | bytes 1048592 | tf_op jit(solution)/shard_map/psum | solution.py:72
  248.8 2.7 bitcast_add_fusion
  251.4 1.4 collective-permute-start
  252.8 10.7 %fusion.6 = f32[16,128,256]{2,0,1:T(8,128)S(1)} fusion(f32[64,128,256]{2,1,0:T(8,128)} %fusion.38, s32[64]{0:T(128)S(1)} %get-tuple-element.5), kind=kOutput, calls=%fused_computation.10 | convolution fusion | flops 402654208 | bytes 10486016 | tf_op jit(solution)/shard_map/mr,mik->rik/dot_general | solution.py:48
  263.5 1.2 copy.8
  264.8 1.3 copy-done.5
  266.5 2.8 gather_fusion.2
  269.3 9.7 %collective-permute-done = f32[1024,256]{1,0:T(8,128)} collective-permute-done((f32[1024,256]{1,0:T(8,128)}, f32[1024,256]{1,0:T(8,128)}, u32[]{:S(2)}, u32[]{:S(2)}) %collective-permute-start) | collective-permute-done | bytes 1048608 | tf_op jit(solution)/shard_map/ppermute | solution.py:21
  279.0 1.3 convert_element_type.47
  280.3 2.8 gather_fusion.3
  283.1 6.1 %fusion.9 = bf16[64,128,128]{2,1,0:T(8,128)(2,1)S(1)} fusion(s32[1,1,2,64,128,128]{5,4,3,2,1,0:T(8,128)} %param.11, bf16[64,128,256]{2,1,0:T(8,128)(2,1)} %gather_fusion.2, bf16[64,128,256]{2,1,0:T(8,128)(2,1)} %gather_fusion.3, pred[64]{0:T(512)(128)(4,1)S(1)} %iota_compare_fusion.4), kind=kOutput, calls=%fused_computation.14 | convolution fusion | flops 543162368 | bytes 14680128 | tf_op jit(solution)/shard_map/mik,mjk->mij/dot_general | solution.py:32
  289.2 1.3 fusion.41
  291.3 4.5 fusion.40
  295.8 7.7 %fusion = f32[8,128,256]{2,0,1:T(8,128)S(1)} fusion(f32[64,128,256]{2,1,0:T(8,128)S(1)} %fusion.41, s32[64]{0:T(128)S(1)} %get-tuple-element.2), kind=kOutput, calls=%fused_computation.4 | convolution fusion | flops 201327104 | bytes 9437440 | tf_op jit(solution)/shard_map/mr,mik->rik/dot_general | solution.py:49
  303.5 1.3 copy.11
  304.8 10.7 %fusion.2 = f32[16,128,256]{2,0,1:T(8,128)S(1)} fusion(f32[64,128,256]{2,1,0:T(8,128)} %fusion.40, s32[64]{0:T(128)S(1)} %get-tuple-element.4), kind=kOutput, calls=%fused_computation.6 | convolution fusion | flops 402654208 | bytes 10486016 | tf_op jit(solution)/shard_map/mr,mik->rik/dot_general | solution.py:48
  315.5 1.2 copy.10
  317.1 1.9 fusion.13
  319.0 159.9 %all-reduce.5.cloned.1.call-done = f32[1024,256]{1,0:T(8,128)} async-done(((f32[1024,256]{1,0:T(8,128)}), f32[1024,256]{1,0:T(8,128)}) %all-reduce.5.cloned.1.call-update) | async-done | bytes 1048592 | tf_op jit(solution)/shard_map/psum | solution.py:72
  478.8 1.5 fusion.20
  (34 shorter events, 3.8 us)
Async XLA Ops:
  7.2 14.7 %copy-start.3 = (f32[2048,256]{1,0:T(8,128)S(1)}, f32[2048,256]{1,0:T(8,128)}, u32[]{:S(2)}) copy-start(f32[2048,256]{1,0:T(8,128)} %param.6) | copy-start | bytes 6291460
  7.2 14.9 %copy-start.8 = (s32[1,1,2,64]{3,2,1,0:T(2,128)S(1)}, s32[1,1,2,64]{3,2,1,0:T(2,128)}, u32[]{:S(2)}) copy-start(s32[1,1,2,64]{3,2,1,0:T(2,128)} %param.8) | copy-start | bytes 1540
  7.2 14.9 %copy-start.7 = (s32[1,1,2,64]{3,2,1,0:T(2,128)S(1)}, s32[1,1,2,64]{3,2,1,0:T(2,128)}, u32[]{:S(2)}) copy-start(s32[1,1,2,64]{3,2,1,0:T(2,128)} %param.9) | copy-start | bytes 1540
  9.3 34.7 %all-to-all-start = ((f32[16,64,256]{2,1,0:T(8,128)}), f32[16,64,256]{2,1,0:T(8,128)}, u32[]{:S(2)}, u32[]{:S(2)}) async-start(f32[16,64,256]{2,1,0:T(8,128)} %stack.2), calls=%async_computation | async-start | bytes 2097152 | tf_op jit(solution)/shard_map/all_to_all | solution.py:10
  21.9 226.9 %all-reduce.3.cloned.1.call-start = ((), (), s32[]{:S(2)}) async-start(), calls=%async_computation.1 | async-start | bytes 2097152 | tf_op jit(solution)/shard_map/psum | solution.py:72
  22.1 2.8 copy-start.9
  48.0 6.1 %copy-start = (bf16[64,128,256]{2,1,0:T(8,128)(2,1)S(1)}, bf16[64,128,256]{2,1,0:T(8,128)(2,1)}, u32[]{:S(2)}) copy-start(bf16[64,128,256]{2,1,0:T(8,128)(2,1)} %gather_fusion) | copy-start | bytes 12582916
  64.2 414.6 %all-reduce.5.cloned.1.call-start = ((), (), s32[]{:S(2)}) async-start(), calls=%async_computation.2 | async-start | bytes 2097152 | tf_op jit(solution)/shard_map/psum | solution.py:72
  251.4 27.5 %collective-permute-start = (f32[1024,256]{1,0:T(8,128)}, f32[1024,256]{1,0:T(8,128)}, u32[]{:S(2)}, u32[]{:S(2)}) collective-permute-start(f32[1024,256]{1,0:T(8,128)} %bitcast_add_fusion), channel_id=1, source_target_pairs={{240,0},{0,16},{16,32},{32,48},{48,64},{64,80},{80,96},{96,112},{1... | collective-permute-start | bytes 3145736 | tf_op jit(solution)/shard_map/ppermute | solution.py:21
  263.5 2.6 copy-start.4
  264.8 1.3 copy-start.5
  283.1 6.1 %copy-start.1 = (bf16[64,128,256]{2,1,0:T(8,128)(2,1)S(1)}, bf16[64,128,256]{2,1,0:T(8,128)(2,1)}, u32[]{:S(2)}) copy-start(bf16[64,128,256]{2,1,0:T(8,128)(2,1)} %gather_fusion.2) | copy-start | bytes 12582916
  289.1 2.2 copy-start.2
  315.5 1.6 copy-start.6
Sparse Core Ops, SparseCore 0:
  64.3 184.3 all-reduce.2
  304.9 173.8 all-reduce.4
